TPU v7x, 32 devices: a whole 2x2x4 slice. The times are simulated.
32 devices in a mesh: grp: 4 (over z), sub: 8 (over y, x, core).
Axes of the slice: x: 2, y: 2, z: 4, core: 2. Of those that a mesh axis runs over, the one named last changes fastest.
Arguments:
- stiff_blocks: float32 [8, 128, 4, 128, 128], P('grp', 'sub'), may hold values from -0.25 to 0.25
- block_cols: int32 [8, 128, 4], P('grp', 'sub'), may hold values from 0 to 127, as said below
- live_blocks: int32 [8, 8], P('grp', 'sub'), may hold values from 1 to 16, as said below
- sub_diag: float32 [8, 16384], P('grp', 'sub'), may hold values from 0.05 to 1
- penalty: float32 [8, 1024], P('grp', 'sub'), may hold values from 0.5 to 4
- sub_load: float32 [8, 16384], P('grp', 'sub'), may hold values from -6 to 6
- iface_map: int32 [8, 1024], P('grp', 'sub'), may hold values from 0 to 262143
- global_load: float32 [1024, 256], P(('grp', 'sub')), may hold values from -6 to 6
- global_diag: float32 [1024, 256], P(('grp', 'sub')), may hold values from 0.1 to 1
Outputs:
- global_field: float32 [1024, 256], P(('grp', 'sub'))
- sub_field: float32 [8, 16384], P('grp', 'sub')
Inputs may be any that keep to these rules, and one draw needn't show every extreme that they name: `live_blocks`: every live count is at least 1 and at most 16; the first submodel holds 16 live block rows on index 0 of sub. `block_cols`: among the blocks of one submodel's block rows on one index of sub, at most 8 have their column block among the block rows of any one index of sub; in every submodel some index of sub receives exactly 8 such blocks from every index of sub.
All inputs are finite; a program needn't handle non-finite values.
Results may differ from a plain program's by a relative error of at most 0.0003.
Values sent between devices are 32-bit elements; how exact they have to be, the bound alone decides.
No kernel may reach another device: no remote copies, remote signals or barrier semaphores. Data moves between devices by JAX's collectives and lax.ppermute only.
A program may use at most 64 MiB of HBM per device.

v0:
```python
import jax
import jax.numpy as jnp
from jax import lax
from jax.sharding import PartitionSpec as P

CG_STEPS = 2
COUPLE = 2
CAP = 8
HIGH = lax.Precision.HIGHEST


def with_halo(x, sides, width):
    for axis, dim in sides:
        peers, length = (lax.axis_size(axis), x.shape[dim])
        up = [(i, (i + 1) % peers) for i in range(peers - 1)]
        down = [(j, i) for i, j in up]
        last = lax.slice_in_dim(x, length - width, length, axis=dim)
        first = lax.slice_in_dim(x, 0, width, axis=dim)
        before = lax.ppermute(last, axis, up)
        after = lax.ppermute(first, axis, down)
        x = jnp.concatenate([before, x, after], axis=dim)
    return x


def glob_apply(field, gdiag):
    padded = with_halo(field, ((("grp", "sub"), 0),), 1)
    padded = jnp.pad(padded, ((0, 0), (1, 1)))
    beside = padded[2:, 1:-1] + padded[:-2, 1:-1] + padded[1:-1, 2:] + padded[1:-1, :-2]
    return (4.0 + gdiag) * field - beside


def row_sum(left, right):
    return jnp.sum(left * right, axis=1, keepdims=True)


def body(
    stiff_blocks,
    block_cols,
    live_blocks,
    sub_diag,
    penalty,
    sub_load,
    iface_map,
    global_load,
    global_diag,
):
    slots = stiff_blocks.shape[0]
    block_rows = stiff_blocks.shape[1]
    width = stiff_blocks.shape[3]
    rows_dev = block_rows * width
    gx_rows, gy_cols = global_load.shape
    glob_local = gx_rows * gy_cols
    groups_sub = lax.axis_size("sub")
    me_flat = lax.axis_index("grp") * groups_sub + lax.axis_index("sub")
    blocks = jnp.arange(rows_dev, dtype=jnp.int32) // width
    mask = (blocks[None, :] < live_blocks).astype(jnp.float32)
    pen_full = jnp.concatenate([penalty, jnp.zeros((slots, rows_dev - width), jnp.float32)], axis=1)
    dsum = sub_diag + pen_full
    flat_cols = block_cols.reshape(slots, -1)
    owner_of = flat_cols // block_rows
    local_of = flat_cols % block_rows
    owner_hot = (owner_of[..., None] == jnp.arange(groups_sub, dtype=jnp.int32)).astype(jnp.int32)
    earlier = jnp.cumsum(owner_hot, axis=1) - owner_hot
    rank_of = jnp.sum(earlier * owner_hot, axis=2)
    bucket_of = owner_of * CAP + rank_of
    placing = (bucket_of[..., None] == jnp.arange(groups_sub * CAP, dtype=jnp.int32)).astype(
        jnp.float32
    )
    send_ids = jnp.einsum("sqk,sq->sk", placing, (local_of + 1).astype(jnp.float32), precision=HIGH)
    send_ids = send_ids.reshape(slots, groups_sub, CAP)

    def sub_apply(vector):
        whole = lax.all_gather(vector, "sub", axis=1, tiled=True)
        tiles = whole.reshape(slots, -1, width)
        picked = jax.vmap(lambda table, index: table[index])(tiles, block_cols)
        strain = jnp.einsum("srnij,srnj->sri", stiff_blocks, picked, precision=HIGH)
        terms = jnp.einsum("srnij,sri->srnj", stiff_blocks, strain, precision=HIGH)
        targets = jnp.arange(block_rows * lax.axis_size("sub"), dtype=jnp.int32)
        onehot = (block_cols[..., None] == targets).astype(jnp.float32)
        back = lax.psum_scatter(
            jnp.einsum("srnm,srnj->msj", onehot, terms, precision=HIGH),
            "sub",
            scatter_dimension=0,
            tiled=True,
        )
        back = jnp.transpose(back, (1, 0, 2)).reshape(slots, rows_dev)
        return mask * (dsum * vector + back)

    all_map = lax.all_gather(iface_map, ("grp", "sub"), axis=0, tiled=True)
    local_idx = all_map - me_flat * glob_local
    valid = (local_idx >= 0) & (local_idx < glob_local)
    seg_idx = jnp.where(valid, local_idx, glob_local)
    global_field = jnp.zeros_like(global_load)
    sub_field = jnp.zeros_like(sub_load)
    for outer in range(COUPLE):
        if outer == 0:
            bvals = jnp.zeros_like(penalty)
        else:
            whole_field = lax.all_gather(global_field, ("grp", "sub"), axis=0, tiled=True)
            bvals = whole_field.reshape(-1)[iface_map]
        b_full = jnp.concatenate([bvals, jnp.zeros((slots, rows_dev - width), jnp.float32)], axis=1)
        rhs = mask * (sub_load + pen_full * b_full)
        field = sub_field
        if outer == 0:
            resid = rhs
        else:
            resid = rhs - sub_apply(field)

        def norm_sum(vector):
            return lax.psum(row_sum(vector, vector), "sub")

        direction = resid
        norm_now = norm_sum(resid)
        for step in range(CG_STEPS):
            image = sub_apply(direction)
            alpha = norm_now / lax.psum(row_sum(direction, image), "sub")
            field = field + alpha * direction
            resid = resid - alpha * image
            if step + 1 < CG_STEPS:
                norm_next = norm_sum(resid)
                direction = resid + norm_next / norm_now * direction
                norm_now = norm_next
        sub_field = field
        lam = penalty * (sub_field[:, :width] - bvals)
        lam_all = lax.all_gather(lam, ("grp", "sub"), axis=0, tiled=True)
        lam_g = jax.ops.segment_sum(
            lam_all.reshape(-1), seg_idx.reshape(-1), num_segments=glob_local + 1
        )
        lam_g = lam_g[:glob_local].reshape(gx_rows, gy_cols)
        if outer == 0:
            resid_g = global_load + lam_g
        else:
            resid_g = global_load - glob_apply(global_field, global_diag) + lam_g
        image_g = glob_apply(resid_g, global_diag)
        top, bottom = lax.psum(
            (jnp.sum(resid_g * resid_g), jnp.sum(resid_g * image_g)), ("grp", "sub")
        )
        global_field = global_field + top / bottom * resid_g
    return (global_field, sub_field)


def solution(mesh):
    return jax.shard_map(
        body,
        mesh=mesh,
        in_specs=(
            P("grp", "sub", None, None, None),
            P("grp", "sub", None),
            P("grp", "sub"),
            P("grp", "sub"),
            P("grp", "sub"),
            P("grp", "sub"),
            P("grp", "sub"),
            P(("grp", "sub"), None),
            P(("grp", "sub"), None),
        ),
        out_specs=(P(("grp", "sub"), None), P("grp", "sub")),
        check_vma=False,
    )
```

profile of v0, /device:TPU:12, one launch (start us, length us, event | category | flops | bytes accessed | tf_op | source)
XLA Modules:
  0.0 802.4 jit_solution(16290601400072708618)
XLA Ops:
  7.2 0.7 fusion.45
  8.1 0.8 compare_select_fusion.6
  8.9 9.2 %all_gather.28 = f32[2,16384]{1,0:T(2,128)S(1)} all-gather(f32[2,2048]{1,0:T(2,128)S(1)} %compare_select_fusion.6), channel_id=1, replica_groups=mesh['grp'=4,'sub'=8] {'sub'}, dimensions={1}, use_global_device_ids=true | all-gather | bytes 147456 | tf_op jit(solution)/shard_map/all_gather | solution.py:73
  18.1 1.2 gather_fusion.1
  19.4 10.1 %convolution_bitcast_fusion.9 = f32[2,16,128,1,1]{2,3,4,1,0:T(1,128)S(1)} fusion(f32[2,16,4,128,1]{3,4,2,1,0:T(1,128)S(1)} %bitcast.242, f32[2,16,4,128,128]{4,3,2,1,0:T(8,128)} %param.9), kind=kOutput, calls=%fused_computation.17 | convolution fusion | flops 25165824 | bytes 8470528 | tf_op jit(solution)/shard_map/srnij,srnj->sri/dot_general | solution.py:76
  29.5 4.1 fusion.53
  33.9 0.8 copy.19
  34.8 30.8 %all-gather = s32[32,2,128]{2,1,0:T(2,128)S(1)} all-gather(s32[1,2,128]{2,1,0:T(2,128)S(1)} %bitcast.257), channel_id=1, replica_groups=mesh['grp'=4,'sub'=8] {'grp','sub'}, dimensions={0}, use_global_device_ids=true | all-gather | bytes 33792 | tf_op jit(solution)/shard_map/all_gather | solution.py:89
  66.8 20.5 %all-reduce.20.cloned.1.call-done = f32[128,2,128]{2,1,0:T(2,128)} async-done(((f32[128,2,128]{2,1,0:T(2,128)}), f32[128,2,128]{2,1,0:T(2,128)}) %all-reduce.20.cloned.1.call-update) | async-done | bytes 131088
  87.3 0.9 multiply_reduce_fusion.6
  88.3 11.8 %all-reduce.13 = (f32[2,1]{0,1:T(1,128)S(1)}, f32[2,1]{0,1:T(1,128)S(1)}) all-reduce(f32[2,1]{0,1:T(1,128)S(1)} %bitcast.259, f32[2,1]{0,1:T(1,128)S(1)} %bitcast.258), channel_id=1, replica_groups=mesh['grp'=4,'sub'=8] {'sub'}, use_global_device_ids=true, to_apply=%region_1.2 | all-reduce | flops 4 | bytes 32 | tf_op jit(solution)/shard_map/psum | solution.py:110
  100.3 11.8 %psum.86 = f32[2,1]{0,1:T(1,128)S(1)} all-reduce(f32[2,1]{0,1:T(1,128)S(1)} %bitcast.264), channel_id=1, replica_groups=mesh['grp'=4,'sub'=8] {'sub'}, use_global_device_ids=true, to_apply=%region_6.7 | all-reduce | flops 2 | bytes 16 | tf_op jit(solution)/shard_map/psum | solution.py:110
  112.2 9.3 %all_gather.29 = f32[2,16384]{1,0:T(2,128)S(1)} all-gather(f32[2,2048]{1,0:T(2,128)S(1)} %multiply_add_fusion.4), channel_id=1, replica_groups=mesh['grp'=4,'sub'=8] {'sub'}, dimensions={1}, use_global_device_ids=true | all-gather | bytes 147456 | tf_op jit(solution)/shard_map/all_gather | solution.py:73
  121.5 1.2 gather_fusion.2
  122.8 9.2 %convolution_bitcast_fusion.8 = f32[2,16,128,1,1]{2,3,4,1,0:T(1,128)S(1)} fusion(f32[2,16,4,128,1]{3,4,2,1,0:T(1,128)S(1)} %bitcast.243, f32[2,16,4,128,128]{4,3,2,1,0:T(8,128)} %param.9), kind=kOutput, calls=%fused_computation.16 | convolution fusion | flops 25165824 | bytes 8470528 | tf_op jit(solution)/shard_map/srnij,srnj->sri/dot_general | solution.py:76
  132.0 6.4 fusion.54
  138.7 0.8 copy.20
  139.6 52.7 %all-reduce.22.cloned.1.call-done = f32[128,2,128]{2,1,0:T(2,128)} async-done(((f32[128,2,128]{2,1,0:T(2,128)}), f32[128,2,128]{2,1,0:T(2,128)}) %all-reduce.22.cloned.1.call-update) | async-done | bytes 131088
  192.2 0.9 fusion.38
  193.2 11.8 %psum.87 = f32[2,1]{0,1:T(1,128)S(1)} all-reduce(f32[2,1]{0,1:T(1,128)S(1)} %bitcast.263), channel_id=1, replica_groups=mesh['grp'=4,'sub'=8] {'sub'}, use_global_device_ids=true, to_apply=%region_9.10 | all-reduce | flops 2 | bytes 16 | tf_op jit(solution)/shard_map/psum | solution.py:116
  205.1 29.1 %all-gather.1 = f32[32,2,128]{2,1,0:T(2,128)S(1)} all-gather(f32[1,2,128]{2,1,0:T(2,128)S(1)} %fusion.49), channel_id=1, replica_groups=mesh['grp'=4,'sub'=8] {'grp','sub'}, dimensions={0}, use_global_device_ids=true | all-gather | bytes 33792 | tf_op jit(solution)/shard_map/all_gather | solution.py:125
  234.2 55.2 %scatter_custom_fusion = f32[8193]{0:T(1024)S(1)} fusion(s32[8192]{0:T(1024)S(1)} %select_bitcast_fusion, f32[8192]{0:T(1024)S(1)} %bitcast.249, f32[]{:T(128)} %constant.41.clone.1), kind=kCustom, calls=%fused_computation.88 | custom fusion | flops 8192 | bytes 32776 | tf_op jit(solution)/shard_map/scatter-add | solution.py:126
  289.5 2.2 collective-permute-start.1
  291.7 5.1 collective-permute-start
  296.8 1.3 collective-permute-done
  298.2 0.7 fusion.21
  298.9 46.9 %all-reduce.11 = (f32[]{:T(128)}, f32[]{:T(128)}) all-reduce(f32[]{:T(128)} %get-tuple-element.5, f32[]{:T(128)} %get-tuple-element.4), channel_id=1, replica_groups=mesh['grp'=4,'sub'=8] {'grp','sub'}, use_global_device_ids=true, to_apply=%region_12.13 | all-reduce | flops 2 | bytes 16 | tf_op jit(solution)/shard_map/psum | solution.py:135
  347.9 8.8 %all_gather.32 = f32[2,16384]{1,0:T(2,128)S(1)} all-gather(f32[2,2048]{1,0:T(2,128)S(1)} %multiply_add_fusion.3), channel_id=1, replica_groups=mesh['grp'=4,'sub'=8] {'sub'}, dimensions={1}, use_global_device_ids=true | all-gather | bytes 147456 | tf_op jit(solution)/shard_map/all_gather | solution.py:73
  356.6 1.2 gather_fusion.3
  357.9 9.2 %convolution_bitcast_fusion.7 = f32[2,16,128,1,1]{2,3,4,1,0:T(1,128)S(1)} fusion(f32[2,16,4,128,1]{3,4,2,1,0:T(1,128)S(1)} %bitcast.244, f32[2,16,4,128,128]{4,3,2,1,0:T(8,128)} %param.9), kind=kOutput, calls=%fused_computation.15 | convolution fusion | flops 25165824 | bytes 8470528 | tf_op jit(solution)/shard_map/srnij,srnj->sri/dot_general | solution.py:76
  367.1 6.4 fusion.55
  373.8 0.8 copy.21
  374.6 24.8 %all-gather.5.cloned.1.call-done = f32[1024,256]{1,0:T(8,128)} async-done(((f32[32,256]{1,0:T(8,128)}), f32[1024,256]{1,0:T(8,128)}) %all-gather.5.cloned.1.call-update) | async-done | bytes 1048592 | tf_op jit(solution)/shard_map/all_gather | solution.py:99
  399.4 1.8 copy.51
  401.2 1.7 gather_fusion
  402.9 51.4 %all-reduce.24.cloned.1.call-done = f32[128,2,128]{2,1,0:T(2,128)} async-done(((f32[128,2,128]{2,1,0:T(2,128)}), f32[128,2,128]{2,1,0:T(2,128)}) %all-reduce.24.cloned.1.call-update) | async-done | bytes 131088
  454.4 0.8 fusion.35
  455.2 9.1 %all_gather.33 = f32[2,16384]{1,0:T(2,128)S(1)} all-gather(f32[2,2048]{1,0:T(2,128)S(1)} %fusion.35), channel_id=1, replica_groups=mesh['grp'=4,'sub'=8] {'sub'}, dimensions={1}, use_global_device_ids=true | all-gather | bytes 147456 | tf_op jit(solution)/shard_map/all_gather | solution.py:73
  464.3 1.2 gather_fusion.4
  465.5 9.2 %convolution_bitcast_fusion.6 = f32[2,16,128,1,1]{2,3,4,1,0:T(1,128)S(1)} fusion(f32[2,16,4,128,1]{3,4,2,1,0:T(1,128)S(1)} %bitcast.245, f32[2,16,4,128,128]{4,3,2,1,0:T(8,128)} %param.9), kind=kOutput, calls=%fused_computation.14 | convolution fusion | flops 25165824 | bytes 8470528 | tf_op jit(solution)/shard_map/srnij,srnj->sri/dot_general | solution.py:76
  474.7 6.4 fusion.56
  481.4 0.8 copy.22
  482.3 2.3 collective-permute-start.3
  484.5 4.2 collective-permute-start.2
  488.8 46.2 %all-reduce.26.cloned.1.call-done = f32[128,2,128]{2,1,0:T(2,128)} async-done(((f32[128,2,128]{2,1,0:T(2,128)}), f32[128,2,128]{2,1,0:T(2,128)}) %all-reduce.26.cloned.1.call-update) | async-done | bytes 131088
  535.0 0.9 multiply_reduce_fusion.3
  535.9 11.8 %all-reduce.12 = (f32[2,1]{0,1:T(1,128)S(1)}, f32[2,1]{0,1:T(1,128)S(1)}) all-reduce(f32[2,1]{0,1:T(1,128)S(1)} %bitcast.261, f32[2,1]{0,1:T(1,128)S(1)} %bitcast.260), channel_id=1, replica_groups=mesh['grp'=4,'sub'=8] {'sub'}, use_global_device_ids=true, to_apply=%region_17.18 | all-reduce | flops 4 | bytes 32 | tf_op jit(solution)/shard_map/psum | solution.py:110
  547.9 11.8 %psum.92 = f32[2,1]{0,1:T(1,128)S(1)} all-reduce(f32[2,1]{0,1:T(1,128)S(1)} %bitcast.265), channel_id=1, replica_groups=mesh['grp'=4,'sub'=8] {'sub'}, use_global_device_ids=true, to_apply=%region_22.23 | all-reduce | flops 2 | bytes 16 | tf_op jit(solution)/shard_map/psum | solution.py:110
  559.8 9.1 %all_gather.34 = f32[2,16384]{1,0:T(2,128)S(1)} all-gather(f32[2,2048]{1,0:T(2,128)S(1)} %multiply_add_fusion.2), channel_id=1, replica_groups=mesh['grp'=4,'sub'=8] {'sub'}, dimensions={1}, use_global_device_ids=true | all-gather | bytes 147456 | tf_op jit(solution)/shard_map/all_gather | solution.py:73
  569.0 1.2 gather_fusion.5
  570.2 9.2 %convolution_bitcast_fusion.5 = f32[2,16,128,1,1]{2,3,4,1,0:T(1,128)S(1)} fusion(f32[2,16,4,128,1]{3,4,2,1,0:T(1,128)S(1)} %bitcast.241, f32[2,16,4,128,128]{4,3,2,1,0:T(8,128)} %param.9), kind=kOutput, calls=%fused_computation.13 | convolution fusion | flops 25165824 | bytes 8470528 | tf_op jit(solution)/shard_map/srnij,srnj->sri/dot_general | solution.py:76
  579.4 6.4 fusion.57
  586.1 0.8 copy.23
  587.0 52.6 %all-reduce.28.cloned.1.call-done = f32[128,2,128]{2,1,0:T(2,128)} async-done(((f32[128,2,128]{2,1,0:T(2,128)}), f32[128,2,128]{2,1,0:T(2,128)}) %all-reduce.28.cloned.1.call-update) | async-done | bytes 131088
  639.7 0.9 fusion.37
  640.6 11.8 %psum.93 = f32[2,1]{0,1:T(1,128)S(1)} all-reduce(f32[2,1]{0,1:T(1,128)S(1)} %bitcast.262), channel_id=1, replica_groups=mesh['grp'=4,'sub'=8] {'sub'}, use_global_device_ids=true, to_apply=%region_25.26 | all-reduce | flops 2 | bytes 16 | tf_op jit(solution)/shard_map/psum | solution.py:116
  652.5 29.1 %all-gather.2 = f32[32,2,128]{2,1,0:T(2,128)S(1)} all-gather(f32[1,2,128]{2,1,0:T(2,128)S(1)} %fusion.48), channel_id=1, replica_groups=mesh['grp'=4,'sub'=8] {'grp','sub'}, dimensions={0}, use_global_device_ids=true | all-gather | bytes 33792 | tf_op jit(solution)/shard_map/all_gather | solution.py:125
  681.6 55.2 %scatter_custom_fusion.1 = f32[8193]{0:T(1024)S(1)} fusion(s32[8192]{0:T(1024)S(1)} %select_bitcast_fusion, f32[8192]{0:T(1024)S(1)} %bitcast.248, f32[]{:T(128)} %constant.41.clone.1), kind=kCustom, calls=%fused_computation.86 | custom fusion | flops 8192 | bytes 32776 | tf_op jit(solution)/shard_map/scatter-add | solution.py:126
  737.0 2.2 collective-permute-start.5
  739.2 5.1 collective-permute-start.4
  744.4 1.3 collective-permute-done.4
  745.7 0.8 fusion.13
  746.5 46.9 %all-reduce.10 = (f32[]{:T(128)}, f32[]{:T(128)}) all-reduce(f32[]{:T(128)} %get-tuple-element.3, f32[]{:T(128)} %get-tuple-element.2), channel_id=1, replica_groups=mesh['grp'=4,'sub'=8] {'grp','sub'}, use_global_device_ids=true, to_apply=%region_28.29 | all-reduce | flops 2 | bytes 16 | tf_op jit(solution)/shard_map/psum | solution.py:135
  794.7 0.6 multiply_add_fusion
  (85 shorter events, 4.7 us)
Async XLA Ops:
  7.2 80.2 %all-reduce.20.cloned.1.call-start = ((), (), s32[]{:S(2)}) async-start(), calls=%async_computation.1 | async-start | bytes 262144
  19.4 10.2 %copy-start = (f32[2,16,4,128,128]{4,3,2,1,0:T(8,128)S(1)}, f32[2,16,4,128,128]{4,3,2,1,0:T(8,128)}, u32[]{:S(2)}) copy-start(f32[2,16,4,128,128]{4,3,2,1,0:T(8,128)} %param.9) | copy-start | bytes 25165828
  19.4 14.2 %copy-start.4 = (s32[2,16,4]{1,2,0:T(4,128)S(1)}, s32[2,16,4]{1,2,0:T(4,128)}, u32[]{:S(2)}) copy-start(s32[2,16,4]{1,2,0:T(4,128)} %param.10) | copy-start | bytes 1540
  19.4 15.4 %copy-start.10 = (s32[2,128]{1,0:T(2,128)S(1)}, s32[2,128]{1,0:T(2,128)}, u32[]{:S(2)}) copy-start(s32[2,128]{1,0:T(2,128)} %param.15) | copy-start | bytes 3076
  19.4 46.2 %copy-start.11 = (u32[32]{0:T(128)S(1)}, u32[32]{0:T(128)}, u32[]{:S(2)}) copy-start(u32[32]{0:T(128)} %constant.138) | copy-start | bytes 388
  19.4 67.9 %copy-start.2 = (f32[2,2048]{1,0:T(2,128)S(1)}, f32[2,2048]{1,0:T(2,128)}, u32[]{:S(2)}) copy-start(f32[2,2048]{1,0:T(2,128)} %param.12) | copy-start | bytes 49156
  19.4 67.9 %copy-start.6 = (f32[2,128]{1,0:T(2,128)S(1)}, f32[2,128]{1,0:T(2,128)}, u32[]{:S(2)}) copy-start(f32[2,128]{1,0:T(2,128)} %param.13) | copy-start | bytes 3076
  19.4 67.9 %copy-start.9 = (s32[2,1]{0,1:T(1,128)S(1)}, s32[2,1]{0,1:T(1,128)}, u32[]{:S(2)}) copy-start(s32[2,1]{0,1:T(1,128)} %param.11) | copy-start | bytes 28
  34.7 157.6 %all-reduce.22.cloned.1.call-start = ((), (), s32[]{:S(2)}) async-start(), calls=%async_computation.2 | async-start | bytes 262144
  122.8 166.7 %copy-start.5 = (f32[32,256]{1,0:T(8,128)S(1)}, f32[32,256]{1,0:T(8,128)}, u32[]{:S(2)}) copy-start(f32[32,256]{1,0:T(8,128)} %param.16) | copy-start | bytes 98308
  122.8 175.4 %copy-start.3 = (f32[32,256]{1,0:T(8,128)S(1)}, f32[32,256]{1,0:T(8,128)}, u32[]{:S(2)}) copy-start(f32[32,256]{1,0:T(8,128)} %param.17) | copy-start | bytes 98308
  139.5 259.9 %all-gather.5.cloned.1.call-start = ((), (), s32[]{:S(2)}) async-start(), calls=%async_computation | async-start | bytes 1081344 | tf_op jit(solution)/shard_map/all_gather | solution.py:99
  289.5 7.4 collective-permute-start.1
  291.7 6.4 collective-permute-start
  347.8 106.6 %all-reduce.24.cloned.1.call-start = ((), (), s32[]{:S(2)}) async-start(), calls=%async_computation.3 | async-start | bytes 262144
  357.9 96.5 %copy-start.7 = (f32[2,2048]{1,0:T(2,128)S(1)}, f32[2,2048]{1,0:T(2,128)}, u32[]{:S(2)}) copy-start(f32[2,2048]{1,0:T(2,128)} %param.14) | copy-start | bytes 49156
  374.6 160.4 %all-reduce.26.cloned.1.call-start = ((), (), s32[]{:S(2)}) async-start(), calls=%async_computation.4 | async-start | bytes 262144
  465.5 16.8 %copy-start.1 = (f32[32,256]{1,0:T(8,128)S(1)}, f32[32,256]{1,0:T(8,128)}, u32[]{:S(2)}) copy-start(f32[32,256]{1,0:T(8,128)} %broadcast_multiply_fusion) | copy-start | bytes 98308
  482.2 157.4 %all-reduce.28.cloned.1.call-start = ((), (), s32[]{:S(2)}) async-start(), calls=%async_computation.5 | async-start | bytes 262144
  482.3 104.6 %collective-permute-start.3 = (f32[1,256]{1,0:T(1,128)S(1)}, f32[1,256]{1,0:T(1,128)S(1)}, u32[]{:S(2)}, u32[]{:S(2)}) collective-permute-start(f32[1,256]{1,0:T(1,128)S(1)} %get-tuple-element.22), channel_id=1, source_target_pairs={{0,1},{1,2},{2,3},{3,4},{4,5},{5,6},{6,7},{7,8},{8,9},{9,10},{10,1... | collective-permute-start | bytes 3080 | tf_op jit(solution)/shard_map/ppermute | solution.py:19
  484.5 102.4 %collective-permute-start.2 = (f32[1,256]{1,0:T(1,128)S(1)}, f32[1,256]{1,0:T(1,128)S(1)}, u32[]{:S(2)}, u32[]{:S(2)}) collective-permute-start(f32[1,256]{1,0:T(1,128)S(1)} %get-tuple-element.23), channel_id=1, source_target_pairs={{1,0},{2,1},{3,2},{4,3},{5,4},{6,5},{7,6},{8,7},{9,8},{10,9},{11,1... | collective-permute-start | bytes 3080 | tf_op jit(solution)/shard_map/ppermute | solution.py:20
  652.5 142.8 %copy-start.8 = (f32[2,2048]{1,0:T(2,128)}, f32[2,2048]{1,0:T(2,128)S(1)}, u32[]{:S(2)}) copy-start(f32[2,2048]{1,0:T(2,128)S(1)} %multiply_add_fusion.1) | copy-start | bytes 49156
  737.0 7.4 collective-permute-start.5
  739.2 6.4 collective-permute-start.4
Sparse Core Ops, SparseCore 0:
  34.8 52.4 all-reduce.19
  139.6 52.5 all-reduce.21
  347.9 51.4 all-gather.4
  402.3 51.9 all-reduce.23
  482.3 52.5 all-reduce.25
  587.0 52.5 all-reduce.27
where the time goes:
time: 811 us; the launch traced here: 802 us
  blocking collectives  299 us (37%)
  waiting for transfers between devices  251 us (31%)
  other arithmetic  120 us (15%)
  matrix products  78.1 us (10%)
  starting transfers between devices  21.4 us (3%)
  between operations  18.1 us (2%)
  local copies, waits for them, and re-layouts  14.3 us (2%)
    unnamed x11, waiting for transfers between devices  224 us
    scatter-add x2, other arithmetic, body(): jax.ops.segment_sum(lam_all.reshape(-1), seg_idx.reshape(-1), num_segment...  110 us
    psum x2, blocking collectives, body(): lax.psum((jnp.sum(resid_g * resid_g), jnp.sum(resid_g * image_g)), ('grp'...  93.8 us
    all_gather x2, blocking collectives, body(): lam_all = lax.all_gather(lam, ('grp', 'sub'), axis=0, tiled=True)  58.2 us
    psum x4, blocking collectives, norm_sum(): return lax.psum(row_sum(vector, vector), 'sub')  47.2 us
    dot_general x5, matrix products, sub_apply(): strain = jnp.einsum('srnij,srnj->sri', stiff_blocks, picked, precision=HIGH)  46.9 us
    all_gather x5, blocking collectives, sub_apply(): whole = lax.all_gather(vector, 'sub', axis=1, tiled=True)  45.5 us
    all_gather x1, blocking collectives, body(): all_map = lax.all_gather(iface_map, ('grp', 'sub'), axis=0, tiled=True)  30.8 us
  transfers between devices with their start and end apart: 12, of which 8 were waited for; matrix products, arithmetic and copies ran while one was open for 5% of the time, Pallas kernels for 0%

commit v1 on v0

--- a/solution.py
+++ b/solution.py
@@ -1,12 +1,21 @@
+import functools
 import jax
 import jax.numpy as jnp
 from jax import lax
 from jax.sharding import PartitionSpec as P
+from jax.lax import all_gather
 
 CG_STEPS = 2
 COUPLE = 2
 CAP = 8
 HIGH = lax.Precision.HIGHEST
+
+
+def unit_group(x_in, axis_key):
+    return all_gather(x_in, axis_key).sum(axis=0)
+
+
+touch_slices = functools.partial(unit_group, axis_key="sub")
 
 
 def with_halo(x, sides, width):
@@ -107,7 +116,7 @@
             resid = rhs - sub_apply(field)
 
         def norm_sum(vector):
-            return lax.psum(row_sum(vector, vector), "sub")
+            return touch_slices(row_sum(vector, vector))
 
         direction = resid
         norm_now = norm_sum(resid)

time: 811 us -> 815 us (level)
    psum x4 -> x0, blocking collectives: 47.2 us -> none  [norm_sum(): return lax.psum(row_sum(vector, vector), 'sub')]
    unnamed x0 -> x2, blocking collectives: none -> 24.1 us
    psum x2 -> x4, blocking collectives: 23.6 us -> 47.2 us  [body(): alpha = norm_now / lax.psum(row_sum(direction, image), 'sub')]
where the time goes in v1:
time: 815 us; the launch traced here: 806 us
  blocking collectives  300 us (37%)
  waiting for transfers between devices  254 us (31%)
  other arithmetic  121 us (15%)
  matrix products  78.1 us (10%)
  starting transfers between devices  19.1 us (2%)
  between operations  18.7 us (2%)
  local copies, waits for them, and re-layouts  15.6 us (2%)
    unnamed x11, waiting for transfers between devices  227 us
    scatter-add x2, other arithmetic, body(): jax.ops.segment_sum(lam_all.reshape(-1), seg_idx.reshape(-1), num_segment...  110 us
    psum x2, blocking collectives, body(): lax.psum((jnp.sum(resid_g * resid_g), jnp.sum(resid_g * image_g)), ('grp'...  93.8 us
    all_gather x2, blocking collectives, body(): lam_all = lax.all_gather(lam, ('grp', 'sub'), axis=0, tiled=True)  58.2 us
    psum x4, blocking collectives, body(): alpha = norm_now / lax.psum(row_sum(direction, image), 'sub')  47.2 us
    dot_general x5, matrix products, sub_apply(): strain = jnp.einsum('srnij,srnj->sri', stiff_blocks, picked, precision=HIGH)  46.9 us
    all_gather x5, blocking collectives, sub_apply(): whole = lax.all_gather(vector, 'sub', axis=1, tiled=True)  45.5 us
    all_gather x1, blocking collectives, body(): all_map = lax.all_gather(iface_map, ('grp', 'sub'), axis=0, tiled=True)  30.8 us
  transfers between devices with their start and end apart: 12, of which 8 were waited for; matrix products, arithmetic and copies ran while one was open for 5% of the time, Pallas kernels for 0%

profile of v1, /device:TPU:12, one launch (start us, length us, event | category | flops | bytes accessed | tf_op | source)
XLA Modules:
  0.0 806.2 jit_solution(9866449710576111617)
XLA Ops:
  7.2 0.7 fusion.45
  8.1 0.8 compare_select_fusion.6
  8.9 9.2 %all_gather.41 = f32[2,16384]{1,0:T(2,128)S(1)} all-gather(f32[2,2048]{1,0:T(2,128)S(1)} %compare_select_fusion.6), channel_id=1, replica_groups=mesh['grp'=4,'sub'=8] {'sub'}, dimensions={1}, use_global_device_ids=true | all-gather | bytes 147456 | tf_op jit(solution)/shard_map/all_gather | solution.py:82
  18.1 1.2 gather_fusion.1
  19.4 10.1 %convolution_bitcast_fusion.9 = f32[2,16,128,1,1]{2,3,4,1,0:T(1,128)S(1)} fusion(f32[2,16,4,128,1]{3,4,2,1,0:T(1,128)S(1)} %bitcast.251, f32[2,16,4,128,128]{4,3,2,1,0:T(8,128)} %param.9), kind=kOutput, calls=%fused_computation.17 | convolution fusion | flops 25165824 | bytes 8470528 | tf_op jit(solution)/shard_map/srnij,srnj->sri/dot_general | solution.py:85
  29.5 4.1 fusion.58
  33.9 0.8 copy.19
  34.8 30.8 %all-gather.4 = s32[32,2,128]{2,1,0:T(2,128)S(1)} all-gather(s32[1,2,128]{2,1,0:T(2,128)S(1)} %bitcast.266), channel_id=1, replica_groups=mesh['grp'=4,'sub'=8] {'grp','sub'}, dimensions={0}, use_global_device_ids=true | all-gather | bytes 33792 | tf_op jit(solution)/shard_map/all_gather | solution.py:98
  67.5 19.9 %all-reduce.24.cloned.1.call-done = f32[128,2,128]{2,1,0:T(2,128)} async-done(((f32[128,2,128]{2,1,0:T(2,128)}), f32[128,2,128]{2,1,0:T(2,128)}) %all-reduce.24.cloned.1.call-update) | async-done | bytes 131088
  87.3 0.9 multiply_reduce_fusion.7
  88.5 11.8 %all-reduce.17 = (f32[2,1]{0,1:T(1,128)S(1)}, f32[16]{0:T(128)S(1)}) all-reduce(f32[2,1]{0,1:T(1,128)S(1)} %bitcast.267, f32[16]{0:T(128)S(1)} %dynamic-update-slice), channel_id=1, replica_groups=mesh['grp'=4,'sub'=8] {'sub'}, use_global_device_ids=true, to_apply=%region_4.5 | all-reduce | flops 18 | bytes 144 | tf_op jit(solution)/shard_map/psum | solution.py:125
  100.9 11.8 %all-reduce.6 = f32[16]{0:T(128)S(1)} all-reduce(f32[16]{0:T(128)S(1)} %dynamic-update-slice.1), channel_id=3, replica_groups=mesh['grp'=4,'sub'=8] {'sub'}, use_global_device_ids=true, to_apply=%add.6 | all-reduce | flops 16 | bytes 128
  112.9 9.3 %all_gather.43 = f32[2,16384]{1,0:T(2,128)S(1)} all-gather(f32[2,2048]{1,0:T(2,128)S(1)} %multiply_add_fusion.4), channel_id=1, replica_groups=mesh['grp'=4,'sub'=8] {'sub'}, dimensions={1}, use_global_device_ids=true | all-gather | bytes 147456 | tf_op jit(solution)/shard_map/all_gather | solution.py:82
  122.2 1.2 gather_fusion.2
  123.5 9.2 %convolution_bitcast_fusion.8 = f32[2,16,128,1,1]{2,3,4,1,0:T(1,128)S(1)} fusion(f32[2,16,4,128,1]{3,4,2,1,0:T(1,128)S(1)} %bitcast.252, f32[2,16,4,128,128]{4,3,2,1,0:T(8,128)} %param.9), kind=kOutput, calls=%fused_computation.16 | convolution fusion | flops 25165824 | bytes 8470528 | tf_op jit(solution)/shard_map/srnij,srnj->sri/dot_general | solution.py:85
  132.7 6.4 fusion.59
  139.4 0.8 copy.20
  140.2 52.7 %all-reduce.26.cloned.1.call-done = f32[128,2,128]{2,1,0:T(2,128)} async-done(((f32[128,2,128]{2,1,0:T(2,128)}), f32[128,2,128]{2,1,0:T(2,128)}) %all-reduce.26.cloned.1.call-update) | async-done | bytes 131088
  192.9 0.9 fusion.38
  193.8 11.8 %psum.57 = f32[2,1]{0,1:T(1,128)S(1)} all-reduce(f32[2,1]{0,1:T(1,128)S(1)} %bitcast.270), channel_id=1, replica_groups=mesh['grp'=4,'sub'=8] {'sub'}, use_global_device_ids=true, to_apply=%region_9.10 | all-reduce | flops 2 | bytes 16 | tf_op jit(solution)/shard_map/psum | solution.py:125
  205.7 29.1 %all-gather.5 = f32[32,2,128]{2,1,0:T(2,128)S(1)} all-gather(f32[1,2,128]{2,1,0:T(2,128)S(1)} %fusion.49), channel_id=1, replica_groups=mesh['grp'=4,'sub'=8] {'grp','sub'}, dimensions={0}, use_global_device_ids=true | all-gather | bytes 33792 | tf_op jit(solution)/shard_map/all_gather | solution.py:134
  234.8 55.2 %scatter_custom_fusion = f32[8193]{0:T(1024)S(1)} fusion(s32[8192]{0:T(1024)S(1)} %select_bitcast_fusion, f32[8192]{0:T(1024)S(1)} %bitcast.258, f32[]{:T(128)} %constant.41.clone.1), kind=kCustom, calls=%fused_computation.88 | custom fusion | flops 8192 | bytes 32776 | tf_op jit(solution)/shard_map/scatter-add | solution.py:135
  290.1 2.2 collective-permute-start.1
  292.4 5.1 collective-permute-start
  297.5 1.3 collective-permute-done
  298.9 0.8 fusion.21
  299.7 46.9 %all-reduce.15 = (f32[]{:T(128)}, f32[]{:T(128)}) all-reduce(f32[]{:T(128)} %get-tuple-element.5, f32[]{:T(128)} %get-tuple-element.4), channel_id=1, replica_groups=mesh['grp'=4,'sub'=8] {'grp','sub'}, use_global_device_ids=true, to_apply=%region_12.13 | all-reduce | flops 2 | bytes 16 | tf_op jit(solution)/shard_map/psum | solution.py:144
  348.5 8.8 %all_gather.46 = f32[2,16384]{1,0:T(2,128)S(1)} all-gather(f32[2,2048]{1,0:T(2,128)S(1)} %multiply_add_fusion.3), channel_id=1, replica_groups=mesh['grp'=4,'sub'=8] {'sub'}, dimensions={1}, use_global_device_ids=true | all-gather | bytes 147456 | tf_op jit(solution)/shard_map/all_gather | solution.py:82
  357.3 1.2 gather_fusion.3
  358.6 9.2 %convolution_bitcast_fusion.7 = f32[2,16,128,1,1]{2,3,4,1,0:T(1,128)S(1)} fusion(f32[2,16,4,128,1]{3,4,2,1,0:T(1,128)S(1)} %bitcast.253, f32[2,16,4,128,128]{4,3,2,1,0:T(8,128)} %param.9), kind=kOutput, calls=%fused_computation.15 | convolution fusion | flops 25165824 | bytes 8470528 | tf_op jit(solution)/shard_map/srnij,srnj->sri/dot_general | solution.py:85
  367.8 6.4 fusion.60
  374.5 0.8 copy.21
  375.3 24.8 %all-gather.9.cloned.1.call-done = f32[1024,256]{1,0:T(8,128)} async-done(((f32[32,256]{1,0:T(8,128)}), f32[1024,256]{1,0:T(8,128)}) %all-gather.9.cloned.1.call-update) | async-done | bytes 1048592 | tf_op jit(solution)/shard_map/all_gather | solution.py:108
  400.1 1.8 copy.51
  401.9 1.7 gather_fusion
  403.6 51.4 %all-reduce.28.cloned.1.call-done = f32[128,2,128]{2,1,0:T(2,128)} async-done(((f32[128,2,128]{2,1,0:T(2,128)}), f32[128,2,128]{2,1,0:T(2,128)}) %all-reduce.28.cloned.1.call-update) | async-done | bytes 131088
  455.0 0.8 fusion.35
  455.8 9.1 %all_gather.48 = f32[2,16384]{1,0:T(2,128)S(1)} all-gather(f32[2,2048]{1,0:T(2,128)S(1)} %fusion.35), channel_id=1, replica_groups=mesh['grp'=4,'sub'=8] {'sub'}, dimensions={1}, use_global_device_ids=true | all-gather | bytes 147456 | tf_op jit(solution)/shard_map/all_gather | solution.py:82
  465.0 1.2 gather_fusion.4
  466.2 9.2 %convolution_bitcast_fusion.6 = f32[2,16,128,1,1]{2,3,4,1,0:T(1,128)S(1)} fusion(f32[2,16,4,128,1]{3,4,2,1,0:T(1,128)S(1)} %bitcast.254, f32[2,16,4,128,128]{4,3,2,1,0:T(8,128)} %param.9), kind=kOutput, calls=%fused_computation.14 | convolution fusion | flops 25165824 | bytes 8470528 | tf_op jit(solution)/shard_map/srnij,srnj->sri/dot_general | solution.py:85
  475.4 6.4 fusion.61
  482.1 0.8 copy.22
  483.0 2.3 collective-permute-start.3
  485.2 50.4 %all-reduce.30.cloned.1.call-done = f32[128,2,128]{2,1,0:T(2,128)} async-done(((f32[128,2,128]{2,1,0:T(2,128)}), f32[128,2,128]{2,1,0:T(2,128)}) %all-reduce.30.cloned.1.call-update) | async-done | bytes 131088
  535.6 0.9 multiply_reduce_fusion.4
  536.8 11.8 %all-reduce.16 = (f32[2,1]{0,1:T(1,128)S(1)}, f32[16]{0:T(128)S(1)}) all-reduce(f32[2,1]{0,1:T(1,128)S(1)} %bitcast.268, f32[16]{0:T(128)S(1)} %dynamic-update-slice.2), channel_id=1, replica_groups=mesh['grp'=4,'sub'=8] {'sub'}, use_global_device_ids=true, to_apply=%region_20.21 | all-reduce | flops 18 | bytes 144 | tf_op jit(solution)/shard_map/psum | solution.py:125
  549.2 1.9 collective-permute-start.2
  551.1 12.3 %all-reduce.8 = f32[16]{0:T(128)S(1)} all-reduce(f32[16]{0:T(128)S(1)} %dynamic-update-slice.3), channel_id=5, replica_groups=mesh['grp'=4,'sub'=8] {'sub'}, use_global_device_ids=true, to_apply=%add.8 | all-reduce | flops 16 | bytes 128
  563.6 9.1 %all_gather.50 = f32[2,16384]{1,0:T(2,128)S(1)} all-gather(f32[2,2048]{1,0:T(2,128)S(1)} %multiply_add_fusion.2), channel_id=1, replica_groups=mesh['grp'=4,'sub'=8] {'sub'}, dimensions={1}, use_global_device_ids=true | all-gather | bytes 147456 | tf_op jit(solution)/shard_map/all_gather | solution.py:82
  572.8 1.2 gather_fusion.5
  574.0 9.2 %convolution_bitcast_fusion.5 = f32[2,16,128,1,1]{2,3,4,1,0:T(1,128)S(1)} fusion(f32[2,16,4,128,1]{3,4,2,1,0:T(1,128)S(1)} %bitcast.250, f32[2,16,4,128,128]{4,3,2,1,0:T(8,128)} %param.9), kind=kOutput, calls=%fused_computation.13 | convolution fusion | flops 25165824 | bytes 8470528 | tf_op jit(solution)/shard_map/srnij,srnj->sri/dot_general | solution.py:85
  583.2 6.4 fusion.62
  589.9 0.8 copy.23
  590.8 52.6 %all-reduce.32.cloned.1.call-done = f32[128,2,128]{2,1,0:T(2,128)} async-done(((f32[128,2,128]{2,1,0:T(2,128)}), f32[128,2,128]{2,1,0:T(2,128)}) %all-reduce.32.cloned.1.call-update) | async-done | bytes 131088
  643.4 0.9 fusion.37
  644.4 11.8 %psum.61 = f32[2,1]{0,1:T(1,128)S(1)} all-reduce(f32[2,1]{0,1:T(1,128)S(1)} %bitcast.269), channel_id=1, replica_groups=mesh['grp'=4,'sub'=8] {'sub'}, use_global_device_ids=true, to_apply=%region_25.26 | all-reduce | flops 2 | bytes 16 | tf_op jit(solution)/shard_map/psum | solution.py:125
  656.3 29.1 %all-gather.6 = f32[32,2,128]{2,1,0:T(2,128)S(1)} all-gather(f32[1,2,128]{2,1,0:T(2,128)S(1)} %fusion.48), channel_id=1, replica_groups=mesh['grp'=4,'sub'=8] {'grp','sub'}, dimensions={0}, use_global_device_ids=true | all-gather | bytes 33792 | tf_op jit(solution)/shard_map/all_gather | solution.py:134
  685.4 55.2 %scatter_custom_fusion.1 = f32[8193]{0:T(1024)S(1)} fusion(s32[8192]{0:T(1024)S(1)} %select_bitcast_fusion, f32[8192]{0:T(1024)S(1)} %bitcast.257, f32[]{:T(128)} %constant.41.clone.1), kind=kCustom, calls=%fused_computation.86 | custom fusion | flops 8192 | bytes 32776 | tf_op jit(solution)/shard_map/scatter-add | solution.py:135
  740.8 2.2 collective-permute-start.5
  743.0 5.1 collective-permute-start.4
  748.1 1.3 collective-permute-done.4
  749.5 0.8 fusion.13
  750.3 46.9 %all-reduce.14 = (f32[]{:T(128)}, f32[]{:T(128)}) all-reduce(f32[]{:T(128)} %get-tuple-element.3, f32[]{:T(128)} %get-tuple-element.2), channel_id=1, replica_groups=mesh['grp'=4,'sub'=8] {'grp','sub'}, use_global_device_ids=true, to_apply=%region_28.29 | all-reduce | flops 2 | bytes 16 | tf_op jit(solution)/shard_map/psum | solution.py:144
  798.4 0.6 multiply_add_fusion
  (101 shorter events, 6.1 us)
Async XLA Ops:
  7.2 80.2 %all-reduce.24.cloned.1.call-start = ((), (), s32[]{:S(2)}) async-start(), calls=%async_computation.1 | async-start | bytes 262144
  19.4 10.2 %copy-start = (f32[2,16,4,128,128]{4,3,2,1,0:T(8,128)S(1)}, f32[2,16,4,128,128]{4,3,2,1,0:T(8,128)}, u32[]{:S(2)}) copy-start(f32[2,16,4,128,128]{4,3,2,1,0:T(8,128)} %param.9) | copy-start | bytes 25165828
  19.4 14.2 %copy-start.4 = (s32[2,16,4]{1,2,0:T(4,128)S(1)}, s32[2,16,4]{1,2,0:T(4,128)}, u32[]{:S(2)}) copy-start(s32[2,16,4]{1,2,0:T(4,128)} %param.10) | copy-start | bytes 1540
  19.4 15.4 %copy-start.10 = (s32[2,128]{1,0:T(2,128)S(1)}, s32[2,128]{1,0:T(2,128)}, u32[]{:S(2)}) copy-start(s32[2,128]{1,0:T(2,128)} %param.15) | copy-start | bytes 3076
  19.4 46.2 %copy-start.11 = (u32[32]{0:T(128)S(1)}, u32[32]{0:T(128)}, u32[]{:S(2)}) copy-start(u32[32]{0:T(128)} %constant.138) | copy-start | bytes 388
  19.4 67.9 %copy-start.2 = (f32[2,2048]{1,0:T(2,128)S(1)}, f32[2,2048]{1,0:T(2,128)}, u32[]{:S(2)}) copy-start(f32[2,2048]{1,0:T(2,128)} %param.12) | copy-start | bytes 49156
  19.4 67.9 %copy-start.6 = (f32[2,128]{1,0:T(2,128)S(1)}, f32[2,128]{1,0:T(2,128)}, u32[]{:S(2)}) copy-start(f32[2,128]{1,0:T(2,128)} %param.13) | copy-start | bytes 3076
  19.4 67.9 %copy-start.9 = (s32[2,1]{0,1:T(1,128)S(1)}, s32[2,1]{0,1:T(1,128)}, u32[]{:S(2)}) copy-start(s32[2,1]{0,1:T(1,128)} %param.11) | copy-start | bytes 28
  34.7 158.2 %all-reduce.26.cloned.1.call-start = ((), (), s32[]{:S(2)}) async-start(), calls=%async_computation.2 | async-start | bytes 262144
  123.5 166.7 %copy-start.5 = (f32[32,256]{1,0:T(8,128)S(1)}, f32[32,256]{1,0:T(8,128)}, u32[]{:S(2)}) copy-start(f32[32,256]{1,0:T(8,128)} %param.16) | copy-start | bytes 98308
  123.5 175.4 %copy-start.3 = (f32[32,256]{1,0:T(8,128)S(1)}, f32[32,256]{1,0:T(8,128)}, u32[]{:S(2)}) copy-start(f32[32,256]{1,0:T(8,128)} %param.17) | copy-start | bytes 98308
  140.2 259.9 %all-gather.9.cloned.1.call-start = ((), (), s32[]{:S(2)}) async-start(), calls=%async_computation | async-start | bytes 1081344 | tf_op jit(solution)/shard_map/all_gather | solution.py:108
  290.1 7.4 collective-permute-start.1
  292.4 6.4 collective-permute-start
  348.5 106.6 %all-reduce.28.cloned.1.call-start = ((), (), s32[]{:S(2)}) async-start(), calls=%async_computation.3 | async-start | bytes 262144
  358.5 96.5 %copy-start.7 = (f32[2,2048]{1,0:T(2,128)S(1)}, f32[2,2048]{1,0:T(2,128)}, u32[]{:S(2)}) copy-start(f32[2,2048]{1,0:T(2,128)} %param.14) | copy-start | bytes 49156
  375.2 160.4 %all-reduce.30.cloned.1.call-start = ((), (), s32[]{:S(2)}) async-start(), calls=%async_computation.4 | async-start | bytes 262144
  466.2 16.8 %copy-start.1 = (f32[32,256]{1,0:T(8,128)S(1)}, f32[32,256]{1,0:T(8,128)}, u32[]{:S(2)}) copy-start(f32[32,256]{1,0:T(8,128)} %broadcast_multiply_fusion) | copy-start | bytes 98308
  482.9 160.5 %all-reduce.32.cloned.1.call-start = ((), (), s32[]{:S(2)}) async-start(), calls=%async_computation.5 | async-start | bytes 262144
  483.0 107.7 %collective-permute-start.3 = (f32[1,256]{1,0:T(1,128)S(1)}, f32[1,256]{1,0:T(1,128)S(1)}, u32[]{:S(2)}, u32[]{:S(2)}) collective-permute-start(f32[1,256]{1,0:T(1,128)S(1)} %get-tuple-element.22), channel_id=1, source_target_pairs={{0,1},{1,2},{2,3},{3,4},{4,5},{5,6},{6,7},{7,8},{8,9},{9,10},{10,1... | collective-permute-start | bytes 3080 | tf_op jit(solution)/shard_map/ppermute | solution.py:28
  549.2 41.5 %collective-permute-start.2 = (f32[1,256]{1,0:T(1,128)S(1)}, f32[1,256]{1,0:T(1,128)S(1)}, u32[]{:S(2)}, u32[]{:S(2)}) collective-permute-start(f32[1,256]{1,0:T(1,128)S(1)} %get-tuple-element.23), channel_id=1, source_target_pairs={{1,0},{2,1},{3,2},{4,3},{5,4},{6,5},{7,6},{8,7},{9,8},{10,9},{11,1... | collective-permute-start | bytes 3080 | tf_op jit(solution)/shard_map/ppermute | solution.py:29
  656.3 142.8 %copy-start.8 = (f32[2,2048]{1,0:T(2,128)}, f32[2,2048]{1,0:T(2,128)S(1)}, u32[]{:S(2)}) copy-start(f32[2,2048]{1,0:T(2,128)S(1)} %multiply_add_fusion.1) | copy-start | bytes 49156
  740.8 7.4 collective-permute-start.5
  743.0 6.4 collective-permute-start.4
Sparse Core Ops, SparseCore 0:
  34.8 52.4 all-reduce.23
  140.3 52.5 all-reduce.25
  348.6 51.4 all-gather.8
  403.0 51.9 all-reduce.27
  483.0 52.5 all-reduce.29
  590.8 52.5 all-reduce.31
